TPU v7x, 32 devices: a whole 2x2x4 slice. The times are simulated.
32 devices in a mesh: dom: 16 (over z, x, core), feat: 2 (over y).
Axes of the slice: x: 2, y: 2, z: 4, core: 2. Of those that a mesh axis runs over, the one named last changes fastest.
Arguments:
- features: bfloat16 [65536, 1024], P('dom', 'feat'), may hold values from -6 to 6
- w_self: bfloat16 [1024, 256], P('feat'), may hold values from -0.1875 to 0.1875
- w_neigh: bfloat16 [1024, 256], P('feat'), may hold values from -0.1875 to 0.1875
- hidden_bias: float32 [256], replicated, may hold values from -3 to 3
- edge_tiles: bfloat16 [16, 102, 128, 128], P('dom'), may hold values from 0 to 0.099609375
- tile_dst: int32 [16, 102], P('dom'), may hold values from 0 to 31, as said below
- tile_src: int32 [16, 102], P('dom'), may hold values from 0 to 47, as said below
- tile_count: int32 [16], P('dom'), may hold values from 12 to 102, as said below
- bound_rows: int32 [16, 256], P('dom'), may hold values from 0 to 4095, as said below
- send_pick: int32 [16, 16, 128], P('dom'), may hold values from 0 to 255, as said below
- cotangent: bfloat16 [65536, 256], P(('dom', 'feat')), may hold values from -0.0234375 to 0.0234375
Outputs:
- hidden: bfloat16 [65536, 256], P(('dom', 'feat'))
- grad_self: bfloat16 [1024, 256], P('feat')
- grad_neigh: bfloat16 [1024, 256], P('feat')
- grad_bias: float32 [256], replicated
Inputs may be any that keep to these rules, and one draw needn't show every extreme that they name: Within a partition the pairs (tile_dst, tile_src) of its 102 slots are distinct. `tile_src`: A source block below 32 is a row tile of the partition itself; block 32 + q is the block received from partition q. Slots from tile_count[p] on are unused. Some partition uses all 102 slots. `bound_rows`: distinct within each partition. Each list send_pick[p, q] has no repeats.
All inputs are finite; a program needn't handle non-finite values.
Results may differ from a plain program's by a relative error of at most 0.009.
The roundings to bfloat16 on the way count: a program that leaves them out, or rounds other values in their place, can miss the bound.
Values may be sent and summed in bfloat16 or wider, within the bound.
A program may use at most 128 MiB of HBM per device.

v0:
```python
import jax
import jax.numpy as jnp
from jax import lax
from jax.sharding import PartitionSpec as P

TILE = 128


def tile_sums(source, local_tiles, dest_list, source_list, live_count, dest_tiles):
    slice_width = source.shape[1]
    blocks = source.reshape(source.shape[0] // TILE, TILE, slice_width)
    picked = jnp.take(blocks, source_list, axis=0)
    products = jnp.einsum("etc,ecf->etf", local_tiles, picked, preferred_element_type=jnp.float32)
    slot_ids = jnp.arange(source_list.shape[0], dtype=jnp.int32)
    live_slots = (slot_ids < live_count).astype(jnp.float32)
    dest_ids = jnp.arange(dest_tiles, dtype=jnp.int32)[:, None]
    onehot = (dest_list[None, :] == dest_ids).astype(jnp.float32) * live_slots[None, :]
    summed = jnp.einsum("de,etf->dtf", onehot, products, precision=lax.Precision.HIGHEST)
    return summed.reshape(dest_tiles * TILE, slice_width).astype(jnp.bfloat16)


def body(
    features,
    w_self,
    w_neigh,
    hidden_bias,
    edge_tiles,
    tile_dst,
    tile_src,
    tile_count,
    bound_rows,
    send_pick,
    cotangent,
):
    part_count = lax.axis_size("dom")
    slice_width = features.shape[1]
    node_rows = features.shape[0]
    boundary = jnp.take(features, bound_rows[0], axis=0)
    everyone = lax.all_gather(boundary, "dom", axis=0, tiled=True)
    pick_lists = lax.all_to_all(send_pick, "dom", split_axis=1, concat_axis=0, tiled=True)
    offsets = (jnp.arange(part_count, dtype=jnp.int32) * boundary.shape[0])[:, None]
    wanted = (pick_lists[:, 0, :] + offsets).reshape(-1)
    received = jnp.take(everyone, wanted, axis=0)
    source = jnp.concatenate([features, received], 0)
    aggregated = tile_sums(
        source, edge_tiles[0], tile_dst[0], tile_src[0], tile_count[0], node_rows // TILE
    )
    stacked = jnp.concatenate([features, aggregated], 1)
    weights = jnp.concatenate([w_self, w_neigh], 0)
    row_block = stacked
    summed = lax.psum_scatter(
        jnp.dot(row_block, weights, preferred_element_type=jnp.float32),
        "feat",
        scatter_dimension=0,
        tiled=True,
    )
    preact = summed + hidden_bias
    hidden = jnp.maximum(preact, 0.0).astype(jnp.bfloat16)
    pre_grad = jnp.where(preact > 0.0, cotangent, jnp.zeros_like(cotangent))
    shard_rows = lax.all_gather(pre_grad, "feat", axis=0, tiled=True)
    row_block = stacked
    product = lax.dot_general(
        row_block, shard_rows, (((0,), (0,)), ((), ())), preferred_element_type=jnp.float32
    )
    all_grads = product
    bias_grad = jnp.sum(shard_rows.astype(jnp.float32), 0)
    all_grads, bias_grad = lax.psum((all_grads, bias_grad), "dom")
    grad_self = all_grads[:slice_width]
    grad_neigh = all_grads[slice_width:]
    return (hidden, grad_self.astype(jnp.bfloat16), grad_neigh.astype(jnp.bfloat16), bias_grad)


def solution(mesh):
    placed = (
        P("dom", "feat"),
        P("feat", None),
        P("feat", None),
        P(),
        P("dom", None, None, None),
        P("dom", None),
        P("dom", None),
        P("dom"),
        P("dom", None),
        P("dom", None, None),
        P(("dom", "feat"), None),
    )
    return jax.shard_map(
        body,
        mesh=mesh,
        in_specs=placed,
        out_specs=(P(("dom", "feat"), None), P("feat", None), P("feat", None), P()),
        check_vma=False,
    )
```

profile of v0, /device:TPU:0, one launch (start us, length us, event | category | flops | bytes accessed | tf_op | source)
XLA Modules:
  0.0 343.9 jit_solution(6246623295148714957)
XLA Ops:
  7.2 0.0 copy-start
  7.2 0.0 all-gather.3.cloned.1.call-start
  7.2 0.8 compare_select_fusion.3
  8.1 0.8 compare_and_fusion.1
  8.9 4.6 %gather_fusion = bf16[256,512]{1,0:T(8,128)(2,1)} fusion(bf16[4096,512]{1,0:T(8,128)(2,1)} %param.11, s32[1024]{0:T(1024)S(1)} %pad_clamp_fusion.1), kind=kCustom, calls=%fused_computation | custom fusion | bytes 525312 | tf_op jit(solution)/shard_map/jit(_take)/gather | solution.py:38
  13.5 1.8 broadcast_select_fusion.1
  15.3 0.0 all-gather.3.cloned.1.call-update
  15.3 7.4 %all-to-all-start = ((s32[1,16,128]{2,0,1:T(1,128)}), s32[1,16,128]{2,0,1:T(1,128)S(1)}, u32[]{:S(2)}, u32[]{:S(2)}) async-start(s32[1,16,128]{2,0,1:T(1,128)} %bitcast.45), calls=%async_computation | async-start | bytes 16384 | tf_op jit(solution)/shard_map/all_to_all | solution.py:40
  22.7 0.0 reduce-scatter.2.cloned.1.call-start
  23.4 0.7 fusion.18
  24.1 0.7 compare_and_fusion.2
  24.7 4.3 %all-to-all-done = s32[1,16,128]{2,0,1:T(1,128)S(1)} async-done(((s32[1,16,128]{2,0,1:T(1,128)}), s32[1,16,128]{2,0,1:T(1,128)S(1)}, u32[]{:S(2)}, u32[]{:S(2)}) %all-to-all-start) | async-done | bytes 8224 | tf_op jit(solution)/shard_map/all_to_all | solution.py:40
  29.1 0.1 compare_and_fusion
  29.1 0.1 add.105
  29.2 39.3 %all-gather.3.cloned.1.call-done = bf16[4096,512]{1,0:T(8,128)(2,1)} async-done(((bf16[256,512]{1,0:T(8,128)(2,1)}), bf16[4096,512]{1,0:T(8,128)(2,1)}) %all-gather.3.cloned.1.call-update) | async-done | bytes 4194320 | tf_op jit(solution)/shard_map/all_gather | solution.py:39
  68.5 12.2 %gather_fusion.1 = bf16[2048,512]{1,0:T(8,128)(2,1)} fusion(bf16[4096,512]{1,0:T(8,128)(2,1)} %all-gather.3.cloned.1.call-done, s32[2048]{0:T(1024)S(1)} %broadcast_clamp_fusion), kind=kCustom, calls=%fused_computation.1 | custom fusion | bytes 4202496 | tf_op jit(solution)/shard_map/jit(_take)/gather | solution.py:43
  80.7 0.0 copy-start.2
  80.7 1.9 broadcast_select_fusion
  82.6 0.9 copy-done.2
  83.5 3.0 pad_maximum_fusion.1
  86.5 10.2 %gather_fusion.2 = bf16[102,128,512]{2,1,0:T(8,128)(2,1)} fusion(bf16[48,128,512]{2,1,0:T(8,128)(2,1)} %bitcast.39, s32[1024]{0:T(1024)S(1)} %pad_clamp_fusion), kind=kCustom, calls=%fused_computation.2 | custom fusion | bytes 26739096 | tf_op jit(solution)/shard_map/jit(_take)/gather | solution.py:12
  96.7 0.0 copy-done
  96.7 13.8 %fusion.3 = f32[102,128,512]{1,2,0:T(8,128)} fusion(bf16[102,128,512]{2,1,0:T(8,128)(2,1)} %gather_fusion.2, pred[102]{0:T(512)(128)(4,1)S(1)} %compare_and_fusion.2, bf16[1,102,128,128]{3,2,1,0:T(8,128)(2,1)S(1)} %copy-done), kind=kOutput, calls=%fused_computation.6 | convolution fusion | flops 1717960704 | bytes 43450472 | tf_op jit(solution)/shard_map/etc,ecf->etf/dot_general | solution.py:13
  110.5 0.0 copy-start.9
  110.5 28.4 %copy.21 = f32[102,128,512]{2,0,1:T(8,128)} copy(f32[102,128,512]{1,2,0:T(8,128)} %fusion.3) | data formatting | bytes 53477376 | tf_op jit(solution)/shard_map/etc,ecf->etf/dot_general | solution.py:13
  139.0 0.0 copy-done.9
  139.0 16.6 %convolution_convert_fusion = bf16[32,128,512]{2,0,1:T(8,128)(2,1)S(1)} fusion(f32[102,128,512]{2,0,1:T(8,128)} %copy.21, f32[102]{0:T(128)S(1)} %compare_convert_fusion, s32[102]{0:T(128)S(1)} %bitcast.48), kind=kOutput, calls=%fused_computation.14 | convolution fusion | flops 2569017856 | bytes 30933808 | tf_op jit(solution)/shard_map/de,etf->dtf/dot_general | solution.py:18
  155.5 0.0 copy-start.3
  155.5 0.0 copy-start.10
  155.6 0.0 copy-start.11
  155.6 2.4 copy.22
  158.0 0.0 copy-start.5
  158.0 2.0 copy-done.5
  159.9 0.0 copy-done.3
  159.9 0.0 copy-done.10
  159.9 0.0 copy-done.11
  159.9 3.9 %fusion.8 = f32[4096,256]{1,0:T(8,128)} fusion(bf16[4096,512]{1,0:T(8,128)(2,1)S(1)} %bitcast.40, bf16[4096,512]{1,0:T(8,128)(2,1)S(1)} %copy-done.3, bf16[512,256]{1,0:T(8,128)(2,1)S(1)} %copy-done.10, bf16[512,256]{1,0:T(8,128)(2,1)S(1)} %copy-done.11), kind=kOutput, calls=%fused_computation.11 | convolution fusion | flops 2165309440 | bytes 13107200 | tf_op jit(solution)/shard_map/dot_general | solution.py:52
  163.8 0.0 copy-start.7
  163.8 0.0 copy-start.8
  163.8 0.0 reduce-scatter.2.cloned.1.call-update
  163.8 0.3 all-gather.5.cloned.1.call-start
  164.1 52.8 %reduce-scatter.2.cloned.1.call-done = f32[2048,256]{1,0:T(8,128)} async-done(((f32[4096,256]{1,0:T(8,128)}), f32[2048,256]{1,0:T(8,128)}) %reduce-scatter.2.cloned.1.call-update) | async-done | bytes 2097168 | tf_op jit(solution)/shard_map/reduce_scatter | solution.py:51
  216.9 0.0 copy-done.7
  216.9 0.0 copy-done.8
  216.9 0.0 copy-start.4
  216.9 3.0 compare_select_fusion
  220.0 0.0 all-gather.5.cloned.1.call-update
  220.0 0.0 copy-done.4
  220.0 1.2 maximum_convert_fusion
  221.2 32.1 %all-gather.5.cloned.1.call-done = bf16[4096,256]{1,0:T(8,128)(2,1)} async-done(((bf16[2048,256]{1,0:T(8,128)(2,1)}), bf16[4096,256]{1,0:T(8,128)(2,1)}) %all-gather.5.cloned.1.call-update) | async-done | bytes 2097168 | tf_op jit(solution)/shard_map/all_gather | solution.py:60
  253.3 0.0 copy-start.6
  253.3 0.0 copy-start.1
  253.3 7.6 %fusion.7 = f32[1024,256]{1,0:T(8,128)} fusion(bf16[4096,256]{1,0:T(8,128)(2,1)} %all-gather.5.cloned.1.call-done, bf16[4096,512]{1,0:T(8,128)(2,1)} %bitcast.41, bf16[4096,512]{1,0:T(8,128)(2,1)} %param.11), kind=kOutput, calls=%fused_computation.10 | convolution fusion | flops 2164260864 | bytes 11534336 | tf_op jit(solution)/shard_map/dot_general | solution.py:62
  260.8 0.0 copy-done.6
  260.8 0.6 convert_reduce_fusion
  261.4 74.1 %all-reduce.2 = (bf16[1024,256]{1,0:T(8,128)(2,1)}, f32[256]{0:T(256)}) all-reduce(f32[1024,256]{1,0:T(8,128)} %fusion.7, f32[256]{0:T(256)S(1)} %convert_reduce_fusion), channel_id=1, replica_groups=mesh['dom'=16,'feat'=2] {'dom'}, use_global_device_ids=true, to_apply=%region_1.2 | all-reduce | flops 262400 | bytes 1574912 | tf_op jit(solution)/shard_map/psum | solution.py:67
  335.5 1.9 fusion.23
  337.4 0.0 copy-done.1
  (6 shorter events, 0.0 us)
Async XLA Ops:
  7.2 89.6 %copy-start = (bf16[1,102,128,128]{3,2,1,0:T(8,128)(2,1)S(1)}, bf16[1,102,128,128]{3,2,1,0:T(8,128)(2,1)}, u32[]{:S(2)}) copy-start(bf16[1,102,128,128]{3,2,1,0:T(8,128)(2,1)} %param.15) | copy-start | bytes 10027012
  7.2 61.4 %all-gather.3.cloned.1.call-start = ((), (), s32[]{:S(2)}) async-start(), calls=%async_computation.2 | async-start | bytes 4456448 | tf_op jit(solution)/shard_map/all_gather | solution.py:39
  15.3 13.8 %all-to-all-start = ((s32[1,16,128]{2,0,1:T(1,128)}), s32[1,16,128]{2,0,1:T(1,128)S(1)}, u32[]{:S(2)}, u32[]{:S(2)}) async-start(s32[1,16,128]{2,0,1:T(1,128)} %bitcast.45), calls=%async_computation | async-start | bytes 16384 | tf_op jit(solution)/shard_map/all_to_all | solution.py:40
  22.7 194.2 %reduce-scatter.2.cloned.1.call-start = ((), (), s32[]{:S(2)}) async-start(), calls=%async_computation.3 | async-start | bytes 6291456 | tf_op jit(solution)/shard_map/reduce_scatter | solution.py:51
  80.7 2.8 copy-start.2
  110.5 28.4 %copy-start.9 = (s32[1,102]{1,0:T(1,128)S(1)}, s32[1,102]{1,0:T(1,128)}, u32[]{:S(2)}) copy-start(s32[1,102]{1,0:T(1,128)} %param.16) | copy-start | bytes 1228
  155.5 4.4 %copy-start.3 = (bf16[4096,512]{1,0:T(8,128)(2,1)S(1)}, bf16[4096,512]{1,0:T(8,128)(2,1)}, u32[]{:S(2)}) copy-start(bf16[4096,512]{1,0:T(8,128)(2,1)} %param.11) | copy-start | bytes 12582916
  155.5 4.4 %copy-start.10 = (bf16[512,256]{1,0:T(8,128)(2,1)S(1)}, bf16[512,256]{1,0:T(8,128)(2,1)}, u32[]{:S(2)}) copy-start(bf16[512,256]{1,0:T(8,128)(2,1)} %param.13) | copy-start | bytes 786436
  155.6 4.4 %copy-start.11 = (bf16[512,256]{1,0:T(8,128)(2,1)S(1)}, bf16[512,256]{1,0:T(8,128)(2,1)}, u32[]{:S(2)}) copy-start(bf16[512,256]{1,0:T(8,128)(2,1)} %param.12) | copy-start | bytes 786436
  158.0 2.0 copy-start.5
  163.8 53.1 %copy-start.7 = (bf16[2048,256]{1,0:T(8,128)(2,1)S(1)}, bf16[2048,256]{1,0:T(8,128)(2,1)}, u32[]{:S(2)}) copy-start(bf16[2048,256]{1,0:T(8,128)(2,1)} %param.21) | copy-start | bytes 3145732
  163.8 53.1 %copy-start.8 = (f32[256]{0:T(256)S(1)}, f32[256]{0:T(256)}, u32[]{:S(2)}) copy-start(f32[256]{0:T(256)} %param.14) | copy-start | bytes 3076
  163.8 89.4 %all-gather.5.cloned.1.call-start = ((), (), s32[]{:S(2)}) async-start(), calls=%async_computation.4 | async-start | bytes 3145728 | tf_op jit(solution)/shard_map/all_gather | solution.py:60
  216.9 3.1 copy-start.4
  253.3 7.6 %copy-start.6 = (bf16[4096,256]{1,0:T(8,128)(2,1)S(1)}, bf16[4096,256]{1,0:T(8,128)(2,1)}, u32[]{:S(2)}) copy-start(bf16[4096,256]{1,0:T(8,128)(2,1)} %all-gather.5.cloned.1.call-done) | copy-start | bytes 6291460
  253.3 84.1 %copy-start.1 = (bf16[1,102,128,128]{3,2,1,0:T(8,128)(2,1)S(1)}, bf16[1,102,128,128]{3,2,1,0:T(8,128)(2,1)}, u32[]{:S(2)}) copy-start(bf16[1,102,128,128]{3,2,1,0:T(8,128)(2,1)} %param.15) | copy-start | bytes 10027012
Sparse Core Ops, SparseCore 0:
  15.4 53.0 all-gather.2
  164.0 52.9 reduce-scatter.1
  220.1 33.1 all-gather.4
where the time goes:
time: 345 us; the launch traced here: 344 us
  waiting for transfers between devices  129 us (37%)
  blocking collectives  74.1 us (21%)
  local copies, waits for them, and re-layouts  62.7 us (18%)
  matrix products  41.8 us (12%)
  other arithmetic  14.5 us (4%)
  between operations  14.5 us (4%)
  starting transfers between devices  7.74 us (2%)
    psum x1, blocking collectives, body(): all_grads, bias_grad = lax.psum((all_grads, bias_grad), 'dom')  74.1 us
    reduce_scatter x1, waiting for transfers between devices, body(): lax.psum_scatter(jnp.dot(row_block, weights, preferred_element_type=jnp.f...  52.8 us
    all_gather x1, waiting for transfers between devices, body(): everyone = lax.all_gather(boundary, 'dom', axis=0, tiled=True)  39.3 us
    all_gather x1, waiting for transfers between devices, body(): shard_rows = lax.all_gather(pre_grad, 'feat', axis=0, tiled=True)  32.1 us
    dot_general x1, local copies, waits for them, and re-layouts, tile_sums(): jnp.einsum('etc,ecf->etf', local_tiles, picked, preferred_element_type=jn...  28.4 us
    dot_general x1, matrix products, tile_sums(): jnp.einsum('de,etf->dtf', onehot, products, precision=lax.Precision.HIGHEST)  16.6 us
    dot_general x1, matrix products, tile_sums(): jnp.einsum('etc,ecf->etf', local_tiles, picked, preferred_element_type=jn...  13.8 us
    gather x1, local copies, waits for them, and re-layouts, body(): received = jnp.take(everyone, wanted, axis=0)  12.2 us
  transfers between devices with their start and end apart: 4, of which 4 were waited for; matrix products, arithmetic and copies ran while one was open for 1% of the time, Pallas kernels for 0%

commit v1 on v0

--- a/solution.py
+++ b/solution.py
@@ -36,7 +36,9 @@
     slice_width = features.shape[1]
     node_rows = features.shape[0]
     boundary = jnp.take(features, bound_rows[0], axis=0)
-    everyone = lax.all_gather(boundary, "dom", axis=0, tiled=True)
+    everyone = jnp.concatenate(
+        lax.all_to_all(jnp.stack([boundary] * lax.axis_size("dom")), "dom", 0, 0), axis=0
+    )
     pick_lists = lax.all_to_all(send_pick, "dom", split_axis=1, concat_axis=0, tiled=True)
     offsets = (jnp.arange(part_count, dtype=jnp.int32) * boundary.shape[0])[:, None]
     wanted = (pick_lists[:, 0, :] + offsets).reshape(-1)

time: 345 us -> 403 us (1.17)
  waiting for transfers between devices: 129 us -> 178 us
  starting transfers between devices: 7.74 us -> 14.2 us
    all_to_all x0 -> x1, waiting for transfers between devices: none -> 76.6 us  [body(): lax.all_to_all(jnp.stack([boundary] * lax.axis_size('dom')), 'dom', 0, 0)]
    all_gather x1 -> x0, waiting for transfers between devices: 39.3 us -> none  [body(): everyone = lax.all_gather(boundary, 'dom', axis=0, tiled=True)]
    reduce_scatter x1, waiting for transfers between devices: 52.8 us -> 69.3 us  [body(): lax.psum_scatter(jnp.dot(row_block, weights, preferred_element_type=jnp.f...]
    all_to_all x0 -> x1, starting transfers between devices: none -> 6.19 us  [body(): lax.all_to_all(jnp.stack([boundary] * lax.axis_size('dom')), 'dom', 0, 0)]
    all_to_all x1, waiting for transfers between devices: 4.32 us -> 0.01 us  [body(): lax.all_to_all(send_pick, 'dom', split_axis=1, concat_axis=0, tiled=True)]
  transfers between devices with their start and end apart: 4 -> 4, of which waited for: 4 -> 3; matrix products, arithmetic and copies ran while one was open for 1% -> 2% of each run, Pallas kernels for 0% -> 0%
where the time goes in v1:
time: 403 us; the launch traced here: 402 us
  waiting for transfers between devices  178 us (44%)
  blocking collectives  74.1 us (18%)
  local copies, waits for them, and re-layouts  66 us (16%)
  matrix products  41.8 us (10%)
  between operations  14.8 us (4%)
  starting transfers between devices  14.2 us (4%)
  other arithmetic  12.9 us (3%)
    all_to_all x1, waiting for transfers between devices, body(): lax.all_to_all(jnp.stack([boundary] * lax.axis_size('dom')), 'dom', 0, 0)  76.6 us
    psum x1, blocking collectives, body(): all_grads, bias_grad = lax.psum((all_grads, bias_grad), 'dom')  74.1 us
    reduce_scatter x1, waiting for transfers between devices, body(): lax.psum_scatter(jnp.dot(row_block, weights, preferred_element_type=jnp.f...  69.3 us
    all_gather x1, waiting for transfers between devices, body(): shard_rows = lax.all_gather(pre_grad, 'feat', axis=0, tiled=True)  32.1 us
    dot_general x1, local copies, waits for them, and re-layouts, tile_sums(): jnp.einsum('etc,ecf->etf', local_tiles, picked, preferred_element_type=jn...  28.4 us
    dot_general x1, matrix products, tile_sums(): jnp.einsum('de,etf->dtf', onehot, products, precision=lax.Precision.HIGHEST)  16.6 us
    dot_general x1, matrix products, tile_sums(): jnp.einsum('etc,ecf->etf', local_tiles, picked, preferred_element_type=jn...  13.8 us
    gather x1, local copies, waits for them, and re-layouts, body(): received = jnp.take(everyone, wanted, axis=0)  12.2 us
  transfers between devices with their start and end apart: 4, of which 3 were waited for; matrix products, arithmetic and copies ran while one was open for 2% of the time, Pallas kernels for 0%

profile of v1, /device:TPU:0, one launch (start us, length us, event | category | flops | bytes accessed | tf_op | source)
XLA Modules:
  0.0 401.9 jit_solution(10324330588477116181)
XLA Ops:
  7.2 0.0 copy-start
  7.2 7.7 %all-to-all-start = ((s32[1,16,128]{2,0,1:T(1,128)}), s32[1,16,128]{2,0,1:T(1,128)S(1)}, u32[]{:S(2)}, u32[]{:S(2)}) async-start(s32[1,16,128]{2,0,1:T(1,128)} %bitcast.46), calls=%async_computation | async-start | bytes 16384 | tf_op jit(solution)/shard_map/all_to_all | solution.py:42
  14.8 0.7 compare_select_fusion.3
  15.5 0.7 compare_and_fusion.1
  16.2 4.6 %gather_fusion = bf16[256,512]{1,0:T(8,128)(2,1)} fusion(bf16[4096,512]{1,0:T(8,128)(2,1)} %param.11, s32[1024]{0:T(1024)S(1)} %pad_clamp_fusion.1), kind=kCustom, calls=%fused_computation | custom fusion | bytes 525312 | tf_op jit(solution)/shard_map/jit(_take)/gather | solution.py:38
  20.9 1.8 broadcast_select_fusion.1
  22.6 0.0 all-to-all-done
  22.6 3.3 stack.2
  26.0 0.0 copy-start.12
  26.0 6.2 %all-to-all-start.1 = ((bf16[16,256,512]{2,1,0:T(8,128)(2,1)}), bf16[16,256,512]{2,1,0:T(8,128)(2,1)}, u32[]{:S(2)}, u32[]{:S(2)}) async-start(bf16[16,256,512]{2,1,0:T(8,128)(2,1)} %stack.2), calls=%async_computation.1 | async-start | bytes 8388608 | tf_op jit(solution)/shard_map/all_to_all | solution.py:40
  32.2 0.0 reduce-scatter.2.cloned.1.call-start
  32.9 0.0 copy-done.12
  32.9 0.1 compare_and_fusion
  33.0 0.1 add.105
  33.1 76.6 %all-to-all-done.1 = bf16[16,256,512]{2,1,0:T(8,128)(2,1)} async-done(((bf16[16,256,512]{2,1,0:T(8,128)(2,1)}), bf16[16,256,512]{2,1,0:T(8,128)(2,1)}, u32[]{:S(2)}, u32[]{:S(2)}) %all-to-all-start.1) | async-done | bytes 4194336 | tf_op jit(solution)/shard_map/all_to_all | solution.py:40
  109.7 12.2 %gather_fusion.1 = bf16[2048,512]{1,0:T(8,128)(2,1)} fusion(bf16[4096,512]{1,0:T(8,128)(2,1)} %bitcast.10, s32[2048]{0:T(1024)S(1)} %broadcast_clamp_fusion), kind=kCustom, calls=%fused_computation.1 | custom fusion | bytes 4202496 | tf_op jit(solution)/shard_map/jit(_take)/gather | solution.py:45
  121.9 0.0 copy-start.2
  121.9 1.9 broadcast_select_fusion
  123.8 0.9 copy-done.2
  124.7 3.0 pad_maximum_fusion.1
  127.7 10.2 %gather_fusion.2 = bf16[102,128,512]{2,1,0:T(8,128)(2,1)} fusion(bf16[48,128,512]{2,1,0:T(8,128)(2,1)} %bitcast.40, s32[1024]{0:T(1024)S(1)} %pad_clamp_fusion), kind=kCustom, calls=%fused_computation.2 | custom fusion | bytes 26739096 | tf_op jit(solution)/shard_map/jit(_take)/gather | solution.py:12
  137.9 0.0 copy-done
  137.9 13.8 %fusion.3 = f32[102,128,512]{1,2,0:T(8,128)} fusion(bf16[102,128,512]{2,1,0:T(8,128)(2,1)} %gather_fusion.2, pred[102]{0:T(512)(128)(4,1)S(1)} %compare_and_fusion.2, bf16[1,102,128,128]{3,2,1,0:T(8,128)(2,1)S(1)} %copy-done), kind=kOutput, calls=%fused_computation.6 | convolution fusion | flops 1717960704 | bytes 43450472 | tf_op jit(solution)/shard_map/etc,ecf->etf/dot_general | solution.py:13
  151.7 0.0 copy-start.9
  151.7 28.4 %copy.21 = f32[102,128,512]{2,0,1:T(8,128)} copy(f32[102,128,512]{1,2,0:T(8,128)} %fusion.3) | data formatting | bytes 53477376 | tf_op jit(solution)/shard_map/etc,ecf->etf/dot_general | solution.py:13
  180.1 0.0 copy-done.9
  180.1 16.6 %convolution_convert_fusion = bf16[32,128,512]{2,0,1:T(8,128)(2,1)S(1)} fusion(f32[102,128,512]{2,0,1:T(8,128)} %copy.21, f32[102]{0:T(128)S(1)} %compare_convert_fusion, s32[102]{0:T(128)S(1)} %bitcast.49), kind=kOutput, calls=%fused_computation.14 | convolution fusion | flops 2569017856 | bytes 30933808 | tf_op jit(solution)/shard_map/de,etf->dtf/dot_general | solution.py:18
  196.7 0.0 copy-start.3
  196.7 0.0 copy-start.10
  196.7 0.0 copy-start.11
  196.7 2.4 copy.22
  199.1 0.0 copy-start.5
  199.1 2.0 copy-done.5
  201.1 0.0 copy-done.3
  201.1 0.0 copy-done.10
  201.1 0.0 copy-done.11
  201.1 3.9 fusion.8
  205.0 0.0 copy-start.7
  205.0 0.0 copy-start.8
  205.0 0.0 reduce-scatter.2.cloned.1.call-update
  205.0 0.3 all-gather.2.cloned.1.call-start
  205.3 69.3 %reduce-scatter.2.cloned.1.call-done = f32[2048,256]{1,0:T(8,128)} async-done(((f32[4096,256]{1,0:T(8,128)}), f32[2048,256]{1,0:T(8,128)}) %reduce-scatter.2.cloned.1.call-update) | async-done | bytes 2097168 | tf_op jit(solution)/shard_map/reduce_scatter | solution.py:53
  274.6 0.0 copy-done.7
  274.6 0.0 copy-done.8
  274.6 0.0 copy-start.4
  274.6 3.0 compare_select_fusion
  277.6 0.0 all-gather.2.cloned.1.call-update
  277.7 0.0 copy-done.4
  277.7 1.2 maximum_convert_fusion
  278.8 32.1 %all-gather.2.cloned.1.call-done = bf16[4096,256]{1,0:T(8,128)(2,1)} async-done(((bf16[2048,256]{1,0:T(8,128)(2,1)}), bf16[4096,256]{1,0:T(8,128)(2,1)}) %all-gather.2.cloned.1.call-update) | async-done | bytes 2097168 | tf_op jit(solution)/shard_map/all_gather | solution.py:62
  310.9 0.0 copy-start.6
  310.9 0.0 copy-start.1
  310.9 7.6 %fusion.7 = f32[1024,256]{1,0:T(8,128)} fusion(bf16[4096,256]{1,0:T(8,128)(2,1)} %all-gather.2.cloned.1.call-done, bf16[4096,512]{1,0:T(8,128)(2,1)} %bitcast.42, bf16[4096,512]{1,0:T(8,128)(2,1)} %param.11), kind=kOutput, calls=%fused_computation.10 | convolution fusion | flops 2164260864 | bytes 11534336 | tf_op jit(solution)/shard_map/dot_general | solution.py:64
  318.5 0.0 copy-done.6
  318.5 0.6 convert_reduce_fusion
  319.0 74.1 %all-reduce.2 = (bf16[1024,256]{1,0:T(8,128)(2,1)}, f32[256]{0:T(256)}) all-reduce(f32[1024,256]{1,0:T(8,128)} %fusion.7, f32[256]{0:T(256)S(1)} %convert_reduce_fusion), channel_id=1, replica_groups=mesh['dom'=16,'feat'=2] {'dom'}, use_global_device_ids=true, to_apply=%region_1.2 | all-reduce | flops 262400 | bytes 1574912 | tf_op jit(solution)/shard_map/psum | solution.py:69
  393.2 1.9 fusion.23
  395.0 0.0 copy-done.1
  (8 shorter events, 0.1 us)
Async XLA Ops:
  7.2 130.7 %copy-start = (bf16[1,102,128,128]{3,2,1,0:T(8,128)(2,1)S(1)}, bf16[1,102,128,128]{3,2,1,0:T(8,128)(2,1)}, u32[]{:S(2)}) copy-start(bf16[1,102,128,128]{3,2,1,0:T(8,128)(2,1)} %param.15) | copy-start | bytes 10027012
  7.2 15.4 %all-to-all-start = ((s32[1,16,128]{2,0,1:T(1,128)}), s32[1,16,128]{2,0,1:T(1,128)S(1)}, u32[]{:S(2)}, u32[]{:S(2)}) async-start(s32[1,16,128]{2,0,1:T(1,128)} %bitcast.46), calls=%async_computation | async-start | bytes 16384 | tf_op jit(solution)/shard_map/all_to_all | solution.py:42
  26.0 6.9 %copy-start.12 = (s32[1,102]{1,0:T(1,128)S(1)}, s32[1,102]{1,0:T(1,128)}, u32[]{:S(2)}) copy-start(s32[1,102]{1,0:T(1,128)} %param.17) | copy-start | bytes 1228
  26.0 83.7 %all-to-all-start.1 = ((bf16[16,256,512]{2,1,0:T(8,128)(2,1)}), bf16[16,256,512]{2,1,0:T(8,128)(2,1)}, u32[]{:S(2)}, u32[]{:S(2)}) async-start(bf16[16,256,512]{2,1,0:T(8,128)(2,1)} %stack.2), calls=%async_computation.1 | async-start | bytes 8388608 | tf_op jit(solution)/shard_map/all_to_all | solution.py:40
  32.2 242.4 %reduce-scatter.2.cloned.1.call-start = ((), (), s32[]{:S(2)}) async-start(), calls=%async_computation.3 | async-start | bytes 6291456 | tf_op jit(solution)/shard_map/reduce_scatter | solution.py:53
  121.9 2.8 copy-start.2
  151.7 28.4 %copy-start.9 = (s32[1,102]{1,0:T(1,128)S(1)}, s32[1,102]{1,0:T(1,128)}, u32[]{:S(2)}) copy-start(s32[1,102]{1,0:T(1,128)} %param.16) | copy-start | bytes 1228
  196.7 4.4 %copy-start.3 = (bf16[4096,512]{1,0:T(8,128)(2,1)S(1)}, bf16[4096,512]{1,0:T(8,128)(2,1)}, u32[]{:S(2)}) copy-start(bf16[4096,512]{1,0:T(8,128)(2,1)} %param.11) | copy-start | bytes 12582916
  196.7 4.4 %copy-start.10 = (bf16[512,256]{1,0:T(8,128)(2,1)S(1)}, bf16[512,256]{1,0:T(8,128)(2,1)}, u32[]{:S(2)}) copy-start(bf16[512,256]{1,0:T(8,128)(2,1)} %param.13) | copy-start | bytes 786436
  196.7 4.4 %copy-start.11 = (bf16[512,256]{1,0:T(8,128)(2,1)S(1)}, bf16[512,256]{1,0:T(8,128)(2,1)}, u32[]{:S(2)}) copy-start(bf16[512,256]{1,0:T(8,128)(2,1)} %param.12) | copy-start | bytes 786436
  199.1 2.0 copy-start.5
  205.0 69.6 %copy-start.7 = (bf16[2048,256]{1,0:T(8,128)(2,1)S(1)}, bf16[2048,256]{1,0:T(8,128)(2,1)}, u32[]{:S(2)}) copy-start(bf16[2048,256]{1,0:T(8,128)(2,1)} %param.21) | copy-start | bytes 3145732
  205.0 69.6 %copy-start.8 = (f32[256]{0:T(256)S(1)}, f32[256]{0:T(256)}, u32[]{:S(2)}) copy-start(f32[256]{0:T(256)} %param.14) | copy-start | bytes 3076
  205.0 105.9 %all-gather.2.cloned.1.call-start = ((), (), s32[]{:S(2)}) async-start(), calls=%async_computation.4 | async-start | bytes 3145728 | tf_op jit(solution)/shard_map/all_gather | solution.py:62
  274.6 3.1 copy-start.4
  310.9 7.6 %copy-start.6 = (bf16[4096,256]{1,0:T(8,128)(2,1)S(1)}, bf16[4096,256]{1,0:T(8,128)(2,1)}, u32[]{:S(2)}) copy-start(bf16[4096,256]{1,0:T(8,128)(2,1)} %all-gather.2.cloned.1.call-done) | copy-start | bytes 6291460
  310.9 84.1 %copy-start.1 = (bf16[1,102,128,128]{3,2,1,0:T(8,128)(2,1)S(1)}, bf16[1,102,128,128]{3,2,1,0:T(8,128)(2,1)}, u32[]{:S(2)}) copy-start(bf16[1,102,128,128]{3,2,1,0:T(8,128)(2,1)} %param.15) | copy-start | bytes 10027012
Sparse Core Ops, SparseCore 0:
  205.1 69.4 reduce-scatter.1
  277.8 33.0 all-gather.1
